TPU v7x, 32 devices: a whole 2x2x4 slice. The times are simulated.
32 devices in a mesh: row: 8 (over z, x), col: 4 (over y, core).
Axes of the slice: x: 2, y: 2, z: 4, core: 2. Of those that a mesh axis runs over, the one named last changes fastest.
Arguments:
- c_matrix: float32 [3072, 3072], P('row', 'col'), may hold values from -6 to 6
- a_upper: bfloat16 [3072, 3072], P('row', 'col'), may hold values from -0.3125 to 0.3125
- b_upper: bfloat16 [3072, 3072], P('row', 'col'), may hold values from -0.3125 to 0.3125
- a_vectors: bfloat16 [3072, 384], P('row'), may hold values from -1 to 2, as said below
- a_inverse: bfloat16 [3072, 384], P('row'), may hold values from -1 to 2, as said below
- b_vectors: bfloat16 [3072, 384], P('row'), may hold values from -1 to 2, as said below
- b_inverse: bfloat16 [3072, 384], P('row'), may hold values from -1 to 2, as said below
- a_values: bfloat16 [3072], P('row'), may hold values from 0.5 to 4
- b_values: bfloat16 [3072], P('row'), may hold values from 0.5 to 4
Outputs:
- overwritten: float32 [3072, 3072], P('row', 'col')
Inputs may be any that keep to these rules, and one draw needn't show every extreme that they name: `a_vectors`: each 384 x 384 tile is an identity matrix plus independent entries of deviation about 0.5 / sqrt(384). `a_inverse`: each 384 x 384 tile is an identity matrix plus independent entries of deviation about 0.5 / sqrt(384). `b_vectors`: each 384 x 384 tile is an identity matrix plus independent entries of deviation about 0.5 / sqrt(384). `b_inverse`: each 384 x 384 tile is an identity matrix plus independent entries of deviation about 0.5 / sqrt(384).
All inputs are finite; a program needn't handle non-finite values.
Results may differ from a plain program's by a relative error of at most 0.012.
Values may be sent and summed in bfloat16 or wider, within the bound.
A program may use at most 64 MiB of HBM per device.

v0:
```python
import jax
import jax.numpy as jnp
from jax import lax
from jax.sharding import PartitionSpec as P

WAVES = 3


def shifted_2(value, axis, steps):
    count = lax.axis_size(axis)
    leading, last = (max(0, -steps), min(count, count - steps))
    return lax.ppermute(value, axis, [(source, source + steps) for source in range(leading, last)])


def from_root(value, axis, source):
    kept = jnp.where(lax.axis_index(axis) == source, value, 0).astype(value.dtype)
    return lax.psum(kept, axis)


def tile_solve(
    residue, left_vectors, left_inverse, left_values, right_vectors, right_inverse, right_values
):
    section_one = jnp.dot(
        left_inverse, residue.astype(jnp.bfloat16), preferred_element_type=jnp.float32
    ).astype(jnp.bfloat16)
    second = jnp.dot(section_one, right_vectors, preferred_element_type=jnp.float32)
    divisor = left_values.astype(jnp.float32)[:, None] + right_values.astype(jnp.float32)[None, :]
    scaled = (second / divisor).astype(jnp.bfloat16)
    section_three = jnp.dot(left_vectors, scaled, preferred_element_type=jnp.float32).astype(
        jnp.bfloat16
    )
    return jnp.dot(section_three, right_inverse, preferred_element_type=jnp.float32)


def shards(
    c_matrix, a_upper, b_upper, a_vectors, a_inverse, b_vectors, b_inverse, a_values, b_values
):
    tile_size = a_vectors.shape[1]
    column_tiles = c_matrix.shape[1] // tile_size
    levels = lax.axis_size("row")
    my_row = lax.axis_index("row")
    my_column = lax.axis_index("col")
    first_column = my_column * column_tiles
    neighbour = shifted_2(a_upper, "col", -1)
    own_rows = (b_upper, b_vectors, b_inverse, b_values)
    above_one = shifted_2((own_rows[0], own_rows[1], own_rows[2], own_rows[3]), "row", 1)
    above_two = shifted_2((own_rows[0], own_rows[1], own_rows[2], own_rows[3]), "row", 2)
    sources = (own_rows, above_one, above_two)
    column_ids = first_column + jnp.arange(column_tiles * tile_size, dtype=jnp.int32) // tile_size
    state = c_matrix
    for offset in range(WAVES - 1, -1, -1):
        b_block, right_vectors, right_inverse, right_values = sources[offset]
        target = my_row - offset
        local_slot = target - first_column
        owns_tile = (local_slot >= 0) & (local_slot < column_tiles)
        slot_index = jnp.clip(local_slot, 0, column_tiles - 1)
        residue = lax.dynamic_slice_in_dim(state, slot_index * tile_size, tile_size, 1)
        solved = tile_solve(
            residue, a_vectors, a_inverse, a_values, right_vectors, right_inverse, right_values
        )
        placed = lax.dynamic_update_slice_in_dim(state, solved, slot_index * tile_size, 1)
        state = jnp.where(owns_tile, placed, state)
        packet = solved.astype(jnp.bfloat16)
        across = from_root(packet, "col", jnp.maximum(target, 0) // column_tiles)
        change = jnp.dot(across, b_block, preferred_element_type=jnp.float32)
        keep_mask = (target >= 0) & (column_ids > target)
        state = state - jnp.where(keep_mask[None, :], change, jnp.float32(0.0))
        down_tiles = []
        for member in range(column_tiles):
            source_row = jnp.minimum(first_column + member + offset, levels - 1)
            down_tiles.append(from_root(packet, "row", source_row))
        for member in range(column_tiles):
            strip_index = member + offset
            if strip_index < column_tiles:
                a_tile = a_upper[:, strip_index * tile_size : (strip_index + 1) * tile_size]
            else:
                shifted = strip_index - column_tiles
                a_tile = neighbour[:, shifted * tile_size : (shifted + 1) * tile_size]
            source_row = first_column + member + offset
            applies = (my_row < source_row) & (source_row < levels)
            change = jnp.dot(a_tile, down_tiles[member], preferred_element_type=jnp.float32)
            lowered = state[:, member * tile_size : (member + 1) * tile_size] - jnp.where(
                applies, change, jnp.float32(0.0)
            )
            state = state.at[:, member * tile_size : (member + 1) * tile_size].set(lowered)
    return state


def solution(mesh):
    placed = (
        P("row", "col"),
        P("row", "col"),
        P("row", "col"),
        P("row", None),
        P("row", None),
        P("row", None),
        P("row", None),
        P("row"),
        P("row"),
    )
    return jax.shard_map(
        shards, mesh=mesh, in_specs=placed, out_specs=P("row", "col"), check_vma=False
    )
```

profile of v0, /device:TPU:4, one launch (start us, length us, event | category | flops | bytes accessed | tf_op | source)
XLA Modules:
  0.0 383.2 jit_solution(3059346060858013844)
XLA Ops:
  6.5 0.0 all-reduce.10.cloned.1.call-start
  6.6 1.3 copy.41
  7.9 3.5 collective-permute-start
  11.4 3.5 collective-permute-start.2
  14.9 3.5 collective-permute-start.1
  18.4 2.0 collective-permute-start.3
  20.5 4.9 %collective-permute-done.1 = bf16[384]{0:T(512)(128)(2,1)S(1)} collective-permute-done((bf16[384]{0:T(512)(128)(2,1)S(1)}, bf16[384]{0:T(512)(128)(2,1)S(1)}, u32[]{:S(2)}, u32[]{:S(2)}) %collective-permute-start.1) | collective-permute-done | bytes 800 | tf_op jit(solution)/shard_map/ppermute | solution.py:12
  25.4 0.8 fusion.20
  26.1 0.8 select_dynamic-update-slice_fusion.2
  26.9 0.9 broadcast_select_fusion.5
  27.9 0.0 all-reduce.20.cloned.1.call-start
  27.9 0.3 copy-done.2
  28.3 1.9 collective-permute-start.4
  30.2 0.0 all-reduce.20.cloned.1.call-update
  30.2 0.0 all-reduce.12.cloned.1.call-start
  30.2 4.1 %collective-permute-start.5 = (bf16[384,384]{1,0:T(8,128)(2,1)}, bf16[384,384]{1,0:T(8,128)(2,1)}, u32[]{:S(2)}, u32[]{:S(2)}) collective-permute-start(bf16[384,384]{1,0:T(8,128)(2,1)} %param.26), channel_id=1, source_target_pairs={{0,4},{4,8},{8,12},{12,16},{16,20},{20,24},{24,28},{1,5},{5,9},{9,... | collective-permute-start | bytes 884744 | tf_op jit(solution)/shard_map/ppermute | solution.py:12
  34.4 3.7 collective-permute-start.6
  38.1 4.2 %collective-permute-start.7 = (bf16[384,384]{1,0:T(8,128)(2,1)S(1)}, bf16[384,384]{1,0:T(8,128)(2,1)}, u32[]{:S(2)}, u32[]{:S(2)}) collective-permute-start(bf16[384,384]{1,0:T(8,128)(2,1)S(1)} %copy-done.4), channel_id=1, source_target_pairs={{0,4},{4,8},{8,12},{12,16},{16,20},{20,24},{24,28},{1,5},{5,9},{9,... | collective-permute-start | bytes 884744 | tf_op jit(solution)/shard_map/ppermute | solution.py:12
  42.3 0.6 compare_reduce_fusion
  42.9 5.2 %collective-permute-start.8 = (bf16[384,768]{1,0:T(8,128)(2,1)}, bf16[384,768]{1,0:T(8,128)(2,1)}, u32[]{:S(2)}, u32[]{:S(2)}) collective-permute-start(bf16[384,768]{1,0:T(8,128)(2,1)} %param.23), channel_id=1, source_target_pairs={{0,4},{4,8},{8,12},{12,16},{16,20},{20,24},{24,28},{1,5},{5,9},{9,... | collective-permute-start | bytes 1769480 | tf_op jit(solution)/shard_map/ppermute | solution.py:12
  48.1 13.2 %all-reduce.10.cloned.1.call-done = bf16[384,384]{1,0:T(8,128)(2,1)} async-done(((bf16[384,384]{1,0:T(8,128)(2,1)}), bf16[384,384]{1,0:T(8,128)(2,1)}) %all-reduce.10.cloned.1.call-update) | async-done | bytes 294928 | tf_op jit(solution)/shard_map/psum | solution.py:17
  61.3 0.8 copy-done.3
  62.1 1.6 fusion.2
  63.7 75.7 %all-reduce.20.cloned.1.call-done = (bf16[384,384]{1,0:T(8,128)(2,1)}, bf16[384,384]{1,0:T(8,128)(2,1)}) async-done(((bf16[384,384]{1,0:T(8,128)(2,1)}, bf16[384,384]{1,0:T(8,128)(2,1)}), (bf16[384,384]{1,0:T(8,128)(2,1)}, bf16[384,384]{1,0:T(8,128)(2,1)})) %all-reduce.20.cloned.1.call-update) | async-done | bytes 589840 | tf_op jit(solution)/shard_map/psum | solution.py:17
  139.5 2.1 fusion.19
  141.6 1.4 fusion.27
  143.1 1.7 fusion.21
  144.8 1.7 select_dynamic-update-slice_fusion.1
  146.6 1.0 broadcast_select_fusion.6
  147.5 0.0 all-reduce.18.cloned.1.call-start
  147.6 0.5 all-reduce.18.cloned.1.call-update
  148.1 0.0 all-reduce.14.cloned.1.call-start
  148.3 29.5 %all-reduce.12.cloned.1.call-done = bf16[384,384]{1,0:T(8,128)(2,1)} async-done(((bf16[384,384]{1,0:T(8,128)(2,1)}), bf16[384,384]{1,0:T(8,128)(2,1)}) %all-reduce.12.cloned.1.call-update) | async-done | bytes 294928 | tf_op jit(solution)/shard_map/psum | solution.py:17
  177.8 1.6 fusion.1
  179.4 76.4 %all-reduce.18.cloned.1.call-done = (bf16[384,384]{1,0:T(8,128)(2,1)}, bf16[384,384]{1,0:T(8,128)(2,1)}) async-done(((bf16[384,384]{1,0:T(8,128)(2,1)}, bf16[384,384]{1,0:T(8,128)(2,1)}), (bf16[384,384]{1,0:T(8,128)(2,1)}, bf16[384,384]{1,0:T(8,128)(2,1)})) %all-reduce.18.cloned.1.call-update) | async-done | bytes 589840 | tf_op jit(solution)/shard_map/psum | solution.py:17
  255.8 2.0 fusion.14
  257.9 1.4 fusion.26
  259.3 1.7 fusion.22
  261.1 0.8 select_dynamic-update-slice_fusion
  261.8 0.9 broadcast_select_fusion.2
  262.8 0.0 all-reduce.16.cloned.1.call-start
  262.8 0.5 all-reduce.16.cloned.1.call-update
  263.4 29.7 %all-reduce.14.cloned.1.call-done = bf16[384,384]{1,0:T(8,128)(2,1)} async-done(((bf16[384,384]{1,0:T(8,128)(2,1)}), bf16[384,384]{1,0:T(8,128)(2,1)}) %all-reduce.14.cloned.1.call-update) | async-done | bytes 294928 | tf_op jit(solution)/shard_map/psum | solution.py:17
  293.1 1.6 fusion
  294.7 76.4 %all-reduce.16.cloned.1.call-done = (bf16[384,384]{1,0:T(8,128)(2,1)}, bf16[384,384]{1,0:T(8,128)(2,1)}) async-done(((bf16[384,384]{1,0:T(8,128)(2,1)}, bf16[384,384]{1,0:T(8,128)(2,1)}), (bf16[384,384]{1,0:T(8,128)(2,1)}, bf16[384,384]{1,0:T(8,128)(2,1)})) %all-reduce.16.cloned.1.call-update) | async-done | bytes 589840 | tf_op jit(solution)/shard_map/psum | solution.py:17
  371.1 2.0 fusion.9
  373.1 1.0 copy-done.1
  374.1 2.2 fusion.5
  (41 shorter events, 0.2 us)
Async XLA Ops:
  6.5 19.6 %copy-start = (bf16[384,384]{1,0:T(8,128)(2,1)S(1)}, bf16[384,384]{1,0:T(8,128)(2,1)}, u32[]{:S(2)}) copy-start(bf16[384,384]{1,0:T(8,128)(2,1)} %param.24) | copy-start | bytes 884740
  6.5 18.8 %copy-start.10 = (bf16[384,384]{1,0:T(8,128)(2,1)S(1)}, bf16[384,384]{1,0:T(8,128)(2,1)}, u32[]{:S(2)}) copy-start(bf16[384,384]{1,0:T(8,128)(2,1)} %param.25) | copy-start | bytes 884740
  6.5 4.9 %copy-start.4 = (bf16[384,384]{1,0:T(8,128)(2,1)S(1)}, bf16[384,384]{1,0:T(8,128)(2,1)}, u32[]{:S(2)}) copy-start(bf16[384,384]{1,0:T(8,128)(2,1)} %param.27) | copy-start | bytes 884740
  6.5 13.9 %copy-start.8 = (bf16[384]{0:T(512)(128)(2,1)S(1)}, bf16[384]{0:T(512)(128)(2,1)}, u32[]{:S(2)}) copy-start(bf16[384]{0:T(512)(128)(2,1)} %param.28) | copy-start | bytes 2308
  6.5 8.4 %copy-start.9 = (bf16[384]{0:T(512)(128)(2,1)S(1)}, bf16[384]{0:T(512)(128)(2,1)}, u32[]{:S(2)}) copy-start(bf16[384]{0:T(512)(128)(2,1)} %param.29) | copy-start | bytes 2308
  6.5 54.7 %all-reduce.10.cloned.1.call-start = ((), (), s32[]{:S(2)}) async-start(), calls=%async_computation | async-start | bytes 589824 | tf_op jit(solution)/shard_map/psum | solution.py:17
  7.9 17.4 %collective-permute-start = (bf16[384,384]{1,0:T(8,128)(2,1)}, bf16[384,384]{1,0:T(8,128)(2,1)S(1)}, u32[]{:S(2)}, u32[]{:S(2)}) collective-permute-start(bf16[384,384]{1,0:T(8,128)(2,1)} %param.26), channel_id=1, source_target_pairs={{0,8},{4,12},{8,16},{12,20},{16,24},{20,28},{1,9},{5,13},{9,17},{1... | collective-permute-start | bytes 884744 | tf_op jit(solution)/shard_map/ppermute | solution.py:12
  11.4 14.7 %collective-permute-start.2 = (bf16[384,384]{1,0:T(8,128)(2,1)S(1)}, bf16[384,384]{1,0:T(8,128)(2,1)S(1)}, u32[]{:S(2)}, u32[]{:S(2)}) collective-permute-start(bf16[384,384]{1,0:T(8,128)(2,1)S(1)} %copy-done.4), channel_id=1, source_target_pairs={{0,8},{4,12},{8,16},{12,20},{16,24},{20,28},{1,9},{5,13},{9,17},{1... | collective-permute-start | bytes 884744 | tf_op jit(solution)/shard_map/ppermute | solution.py:12
  14.9 10.4 %collective-permute-start.1 = (bf16[384]{0:T(512)(128)(2,1)S(1)}, bf16[384]{0:T(512)(128)(2,1)S(1)}, u32[]{:S(2)}, u32[]{:S(2)}) collective-permute-start(bf16[384]{0:T(512)(128)(2,1)S(1)} %copy-done.9), channel_id=1, source_target_pairs={{0,8},{4,12},{8,16},{12,20},{16,24},{20,28},{1,9},{5,13},{9,17},{1... | collective-permute-start | bytes 2312 | tf_op jit(solution)/shard_map/ppermute | solution.py:12
  18.4 42.9 %collective-permute-start.3 = (bf16[384,768]{1,0:T(8,128)(2,1)}, bf16[384,768]{1,0:T(8,128)(2,1)S(1)}, u32[]{:S(2)}, u32[]{:S(2)}) collective-permute-start(bf16[384,768]{1,0:T(8,128)(2,1)} %param.23), channel_id=1, source_target_pairs={{0,8},{4,12},{8,16},{12,20},{16,24},{20,28},{1,9},{5,13},{9,17},{1... | collective-permute-start | bytes 1769480 | tf_op jit(solution)/shard_map/ppermute | solution.py:12
  26.9 1.4 copy-start.2
  27.9 111.6 %all-reduce.20.cloned.1.call-start = ((), (), s32[]{:S(2)}) async-start(), calls=%async_computation.5 | async-start | bytes 1179648 | tf_op jit(solution)/shard_map/psum | solution.py:17
  28.3 35.5 %collective-permute-start.4 = (bf16[384,768]{1,0:T(8,128)(2,1)S(1)}, bf16[384,768]{1,0:T(8,128)(2,1)}, u32[]{:S(2)}, u32[]{:S(2)}) collective-permute-start(bf16[384,768]{1,0:T(8,128)(2,1)S(1)} %copy-done.2), channel_id=1, source_target_pairs={{1,0},{2,1},{3,2},{5,4},{6,5},{7,6},{9,8},{10,9},{11,10},{13,12},{... | collective-permute-start | bytes 1769480 | tf_op jit(solution)/shard_map/ppermute | solution.py:12
  30.2 147.6 %all-reduce.12.cloned.1.call-start = ((), (), s32[]{:S(2)}) async-start(), calls=%async_computation.1 | async-start | bytes 589824 | tf_op jit(solution)/shard_map/psum | solution.py:17
  30.2 112.8 %collective-permute-start.5 = (bf16[384,384]{1,0:T(8,128)(2,1)}, bf16[384,384]{1,0:T(8,128)(2,1)}, u32[]{:S(2)}, u32[]{:S(2)}) collective-permute-start(bf16[384,384]{1,0:T(8,128)(2,1)} %param.26), channel_id=1, source_target_pairs={{0,4},{4,8},{8,12},{12,16},{16,20},{20,24},{24,28},{1,5},{5,9},{9,... | collective-permute-start | bytes 884744 | tf_op jit(solution)/shard_map/ppermute | solution.py:12
  34.4 8.5 %collective-permute-start.6 = (bf16[384]{0:T(512)(128)(2,1)S(1)}, bf16[384]{0:T(512)(128)(2,1)S(1)}, u32[]{:S(2)}, u32[]{:S(2)}) collective-permute-start(bf16[384]{0:T(512)(128)(2,1)S(1)} %copy-done.9), channel_id=1, source_target_pairs={{0,4},{4,8},{8,12},{12,16},{16,20},{20,24},{24,28},{1,5},{5,9},{9,... | collective-permute-start | bytes 2312 | tf_op jit(solution)/shard_map/ppermute | solution.py:12
  38.1 106.7 %collective-permute-start.7 = (bf16[384,384]{1,0:T(8,128)(2,1)S(1)}, bf16[384,384]{1,0:T(8,128)(2,1)}, u32[]{:S(2)}, u32[]{:S(2)}) collective-permute-start(bf16[384,384]{1,0:T(8,128)(2,1)S(1)} %copy-done.4), channel_id=1, source_target_pairs={{0,4},{4,8},{8,12},{12,16},{16,20},{20,24},{24,28},{1,5},{5,9},{9,... | collective-permute-start | bytes 884744 | tf_op jit(solution)/shard_map/ppermute | solution.py:12
  42.9 105.4 %collective-permute-start.8 = (bf16[384,768]{1,0:T(8,128)(2,1)}, bf16[384,768]{1,0:T(8,128)(2,1)}, u32[]{:S(2)}, u32[]{:S(2)}) collective-permute-start(bf16[384,768]{1,0:T(8,128)(2,1)} %param.23), channel_id=1, source_target_pairs={{0,4},{4,8},{8,12},{12,16},{16,20},{20,24},{24,28},{1,5},{5,9},{9,... | collective-permute-start | bytes 1769480 | tf_op jit(solution)/shard_map/ppermute | solution.py:12
  61.3 0.8 copy-start.3
  139.5 2.2 copy-start.5
  141.6 1.5 copy-start.11
  147.5 108.3 %all-reduce.18.cloned.1.call-start = ((), (), s32[]{:S(2)}) async-start(), calls=%async_computation.4 | async-start | bytes 1179648 | tf_op jit(solution)/shard_map/psum | solution.py:17
  148.1 145.0 %all-reduce.14.cloned.1.call-start = ((), (), s32[]{:S(2)}) async-start(), calls=%async_computation.2 | async-start | bytes 589824 | tf_op jit(solution)/shard_map/psum | solution.py:17
  255.8 2.1 copy-start.6
  257.9 1.5 copy-start.12
  262.8 108.3 %all-reduce.16.cloned.1.call-start = ((), (), s32[]{:S(2)}) async-start(), calls=%async_computation.3 | async-start | bytes 1179648 | tf_op jit(solution)/shard_map/psum | solution.py:17
  371.1 3.1 copy-start.7
  373.1 1.0 copy-start.1
Sparse Core Ops, SparseCore 0:
  28.0 33.2 all-reduce.9
  64.7 74.7 all-reduce.19
  147.7 30.1 all-reduce.11
  181.1 74.7 all-reduce.17
  262.9 30.1 all-reduce.13
  296.3 74.6 all-reduce.15
where the time goes:
time: 385 us; the launch traced here: 383 us
  waiting for transfers between devices  307 us (80%)
  starting transfers between devices  31.7 us (8%)
  matrix products  23.6 us (6%)
  between operations  14 us (4%)
    psum x6, waiting for transfers between devices, from_root(): return lax.psum(kept, axis)  301 us
    ppermute x9, starting transfers between devices, shifted_2(): lax.ppermute(value, axis, [(source, source + steps) for source in range(l...  31.5 us
    dot_general x6, matrix products, shards(): jnp.dot(a_tile, down_tiles[member], preferred_element_type=jnp.float32)  11.3 us
  transfers between devices with their start and end apart: 15, of which 7 were waited for; matrix products, arithmetic and copies ran while one was open for 4% of the time, Pallas kernels for 0%

commit v1 on v0

v1 whole, which is shorter than its diff:
```python
import functools

import jax
import jax.numpy as jnp
from jax import lax
from jax.experimental import pallas as pl
from jax.experimental.pallas import tpu as pltpu
from jax.sharding import PartitionSpec as P

WAVES = 3
MEMBERS = 2
CHUNKS = 2
MESH = pl.DeviceIdType.MESH
f32 = jnp.float32
bf16 = jnp.bfloat16


def kernel(
    rows, cols, tile,
    c_hbm, a_hbm, b_hbm, u_hbm, p_hbm, v_hbm, q_hbm, lam_hbm, mu_hbm,
    out_hbm,
    state, abuf, bbuf, pbuf, ubuf, vbuf, qbuf, lam, mu, xr, xc,
    load_sem, out_sem,
    vq_send, vq_fsend, vq_recv,
    a_send, a_recv,
    b_send, b_fsend, b_recv,
    xr_send, xr_recv,
    xc_send, xc_recv,
):
    r = lax.axis_index("row")
    c = lax.axis_index("col")
    even_row = r % 2 == 0
    odd_row = r % 2 == 1
    even_col = c % 2 == 0
    step = tile // CHUNKS

    def dot(left, right):
        return jnp.dot(left, right, preferred_element_type=f32)

    def part(ref, member):
        return ref.at[:, pl.ds(member * tile, tile)]

    loads = []

    def load(source, target):
        copy = pltpu.make_async_copy(source, target, load_sem.at[len(loads)])
        copy.start()
        loads.append(copy)
        return copy

    ld_p = load(p_hbm, pbuf)
    ld_c = [load(part(c_hbm, m), state.at[m]) for m in range(MEMBERS)]
    ld_lam = load(lam_hbm, lam)
    ld_u = load(u_hbm, ubuf)
    ld_a = [load(part(a_hbm, m), abuf.at[m]) for m in range(MEMBERS)]
    ld_v = load(v_hbm, vbuf.at[0])
    ld_q = load(q_hbm, qbuf.at[0])
    ld_mu = load(mu_hbm, mu.at[0])
    ld_b = [load(part(b_hbm, m), bbuf.at[0, m]) for m in range(MEMBERS)]

    barrier = pltpu.get_barrier_semaphore()
    count = jnp.int32(0)
    for d in (-2, -1, 1, 2):
        there = (r + d >= 0) & (r + d < rows)
        count += there.astype(jnp.int32)

        @pl.when(there)
        def _():
            pl.semaphore_signal(barrier, inc=1, device_id=(r + d, c), device_id_type=MESH)

        there = (c + d >= 0) & (c + d < cols)
        count += there.astype(jnp.int32)

        @pl.when(there)
        def _():
            pl.semaphore_signal(barrier, inc=1, device_id=(r, c + d), device_id_type=MESH)

    pl.semaphore_wait(barrier, count)

    sends = []

    def remote(source, target, send, recv, to):
        return pltpu.make_async_remote_copy(
            src_ref=source, dst_ref=target, send_sem=send, recv_sem=recv,
            device_id=to, device_id_type=MESH,
        )

    def push(condition, *copy):
        @pl.when(condition)
        def _():
            remote(*copy).start()

        sends.append((condition, copy))

    def got(target, recv):
        remote(target, target, recv, recv, (r, c)).wait_recv()

    diagonal = c == r // MEMBERS
    sources = (v_hbm, q_hbm, mu_hbm)
    slots = (vbuf, qbuf, mu)
    for t in (2, 1):
        reach = diagonal & (r + t < rows)
        if t == 1:
            reach = reach & even_row
        for k in (0, 2, 1):
            push(reach, sources[k], slots[k].at[t], vq_send.at[t, k], vq_recv.at[t, k], (r + t, c))
    for m in range(MEMBERS):
        push(
            (c > 0) & (r < MEMBERS * c + m),
            part(a_hbm, m), abuf.at[MEMBERS + m], a_send.at[m], a_recv.at[m], (r, c - 1),
        )
    for t in (2, 1):
        for m in range(MEMBERS):
            reach = (MEMBERS * c + m > r) & (r + t < rows)
            if t == 1:
                reach = reach & even_row
            push(
                reach, part(b_hbm, m), bbuf.at[t, m], b_send.at[t, m], b_recv.at[t, m], (r + t, c)
            )

    def owns(s):
        j = r - s
        return (j >= 0) & (j // MEMBERS == c)

    def update(s, m, condition=None):
        j = MEMBERS * c + m
        i = j + s
        below = (i < rows) & (r < i)
        right = (r - s >= 0) & (j > r - s)
        if condition is not None:
            below = below & condition
            right = right & condition

        @pl.when(below)
        def _():
            state[m] = state[m] - dot(abuf[m + s], xc[s, m])

        @pl.when(right)
        def _():
            state[m] = state[m] - dot(xr[s], bbuf[s, m])

    for copy in (ld_p, *ld_c, ld_lam, ld_u):
        copy.wait()

    for s in range(WAVES - 1, -1, -1):
        mine = owns(s)
        m_own = jnp.clip(r - s - MEMBERS * c, 0, MEMBERS - 1)
        if s < WAVES - 1:
            update(s + 1, m_own, mine)
        if s == 0:
            ld_v.wait()
            ld_q.wait()
            ld_mu.wait()

        @pl.when(mine)
        def _():
            first = dot(pbuf[...], state[m_own].astype(bf16)).astype(bf16)
            if s > 0:
                got(vbuf.at[s], vq_recv.at[s, 0])
                got(mu.at[s], vq_recv.at[s, 2])
            second = dot(first, vbuf[s])
            scaled = (second / (lam[...] + mu[s])).astype(bf16)
            third = dot(ubuf[...], scaled).astype(bf16)
            if s > 0:
                got(qbuf.at[s], vq_recv.at[s, 1])
            solved = dot(third, qbuf[s])
            state[m_own] = solved
            xr[s] = solved.astype(bf16)

        for d in (1, 2):
            for h in range(CHUNKS):
                rng = pl.ds(h * step, step)
                push(
                    mine & (r - d >= 0),
                    xr.at[s, rng], xc.at[s, m_own, rng],
                    xc_send.at[s, MEMBERS + d - 1, h], xc_recv.at[s, m_own, h], (r - d, c),
                )
        held = (r - s >= 0) & (c >= (r - s) // MEMBERS)
        comes = (r - s >= 0) & (c > (r - s) // MEMBERS)
        for h in range(CHUNKS):
            rng = pl.ds(h * step, step)

            @pl.when(comes)
            def _():
                got(xr.at[s, rng], xr_recv.at[s, h])

            for d in (1, 2):
                reach = held & (c + d < cols)
                reach = reach & (even_col if d == 2 else (even_col | mine))
                push(
                    reach, xr.at[s, rng], xr.at[s, rng],
                    xr_send.at[s, d - 1, h], xr_recv.at[s, h], (r, c + d),
                )

        if s == WAVES - 1:
            for k in range(3):
                push(
                    mine & odd_row, slots[k].at[2], slots[k].at[1],
                    vq_fsend.at[k], vq_recv.at[1, k], (r - 1, c),
                )
        if s < WAVES - 1:
            for m in range(MEMBERS):
                update(s + 1, m, jnp.logical_not(mine & (m_own == m)))

        for h in range(CHUNKS):
            for m in range(MEMBERS):
                i = MEMBERS * c + m + s
                rng = pl.ds(h * step, step)
                comes = (i < rows) & (r < i)

                @pl.when(comes)
                def _():
                    got(xc.at[s, m, rng], xc_recv.at[s, m, h])

                push(
                    comes & (r - 2 >= 0), xc.at[s, m, rng], xc.at[s, m, rng],
                    xc_send.at[s, m, h], xc_recv.at[s, m, h], (r - 2, c),
                )

        if s == WAVES - 1:
            for copy in ld_a:
                copy.wait()
            for m in range(MEMBERS):
                @pl.when((c + 1 < cols) & (r < MEMBERS * (c + 1) + m))
                def _():
                    got(abuf.at[MEMBERS + m], a_recv.at[m])
        if s > 0:
            for m in range(MEMBERS):
                comes = (r - s >= 0) & (MEMBERS * c + m > r - s)

                @pl.when(comes)
                def _():
                    got(bbuf.at[s, m], b_recv.at[s, m])

                if s == WAVES - 1:
                    push(
                        comes & odd_row, bbuf.at[2, m], bbuf.at[1, m],
                        b_fsend.at[m], b_recv.at[1, m], (r - 1, c),
                    )
        else:
            for copy in ld_b:
                copy.wait()

    outs = []
    for m in range(MEMBERS):
        update(0, m)
        copy = pltpu.make_async_copy(state.at[m], part(out_hbm, m), out_sem.at[m])
        copy.start()
        outs.append(copy)
    for condition, copy in sends:
        @pl.when(condition)
        def _():
            remote(*copy).wait_send()
    for copy in outs:
        copy.wait()


def shards(
    c_matrix, a_upper, b_upper, a_vectors, a_inverse, b_vectors, b_inverse, a_values, b_values
):
    tile = a_vectors.shape[1]
    rows = lax.axis_size("row")
    cols = lax.axis_size("col")
    lam = a_values.astype(f32).reshape(tile, 1)
    mu = b_values.astype(f32).reshape(1, tile)
    dma = pltpu.SemaphoreType.DMA
    return pl.pallas_call(
        functools.partial(kernel, rows, cols, tile),
        out_shape=jax.ShapeDtypeStruct(c_matrix.shape, f32),
        in_specs=[pl.BlockSpec(memory_space=pl.ANY)] * 9,
        out_specs=pl.BlockSpec(memory_space=pl.ANY),
        scratch_shapes=[
            pltpu.VMEM((MEMBERS, tile, tile), f32),
            pltpu.VMEM((2 * MEMBERS, tile, tile), bf16),
            pltpu.VMEM((WAVES, MEMBERS, tile, tile), bf16),
            pltpu.VMEM((tile, tile), bf16),
            pltpu.VMEM((tile, tile), bf16),
            pltpu.VMEM((WAVES, tile, tile), bf16),
            pltpu.VMEM((WAVES, tile, tile), bf16),
            pltpu.VMEM((tile, 1), f32),
            pltpu.VMEM((WAVES, 1, tile), f32),
            pltpu.VMEM((WAVES, tile, tile), bf16),
            pltpu.VMEM((WAVES, MEMBERS, tile, tile), bf16),
            dma((16,)), dma((MEMBERS,)),
            dma((WAVES, 3)), dma((3,)), dma((WAVES, 3)),
            dma((MEMBERS,)), dma((MEMBERS,)),
            dma((WAVES, MEMBERS)), dma((MEMBERS,)), dma((WAVES, MEMBERS)),
            dma((WAVES, 2, CHUNKS)), dma((WAVES, CHUNKS)),
            dma((WAVES, 2 * MEMBERS, CHUNKS)), dma((WAVES, MEMBERS, CHUNKS)),
        ],
        compiler_params=pltpu.CompilerParams(collective_id=0, has_side_effects=True),
    )(c_matrix, a_upper, b_upper, a_vectors, a_inverse, b_vectors, b_inverse, lam, mu)


def solution(mesh):
    placed = (
        P("row", "col"),
        P("row", "col"),
        P("row", "col"),
        P("row", None),
        P("row", None),
        P("row", None),
        P("row", None),
        P("row"),
        P("row"),
    )
    return jax.shard_map(
        shards, mesh=mesh, in_specs=placed, out_specs=P("row", "col"), check_vma=False
    )
```

time: 385 us -> 88.8 us (0.23)
  waiting for transfers between devices: 307 us -> 0 us
  Pallas kernels: 0 us -> 83.6 us
  starting transfers between devices: 31.7 us -> 0 us
  matrix products: 23.6 us -> 0 us
  between operations: 14 us -> 0.01 us
    psum x6 -> x0, waiting for transfers between devices: 301 us -> none  [from_root(): return lax.psum(kept, axis)]
    pallas_call x0 -> x1, Pallas kernels: none -> 83.6 us  [shards(): pl.pallas_call(functools.partial(kernel, rows, cols, tile), out_shape=jax...]
    ppermute x9 -> x0, starting transfers between devices: 31.5 us -> none  [shifted_2(): lax.ppermute(value, axis, [(source, source + steps) for source in range(l...]
    dot_general x15 -> x0, matrix products: 23.6 us -> none  [the longest x6 11.3 us: shards(): jnp.dot(a_tile, down_tiles[member], preferred_element_type=jnp.float32)]
    ppermute x9 -> x0, waiting for transfers between devices: 4.89 us -> none  [shifted_2(): lax.ppermute(value, axis, [(source, source + steps) for source in range(l...]
  transfers between devices with their start and end apart: 15 -> 0, of which waited for: 7 -> 0; matrix products, arithmetic and copies ran while one was open for 4% -> 0% of each run, Pallas kernels for 0% -> 0%
where the time goes in v1:
time: 88.8 us; the launch traced here: 88.7 us
  Pallas kernels  83.6 us (94%)
  local copies, waits for them, and re-layouts  5.08 us (6%)
    pallas_call x1, Pallas kernels, shards(): pl.pallas_call(functools.partial(kernel, rows, cols, tile), out_shape=jax...  83.6 us
    unnamed x1, local copies, waits for them, and re-layouts  2.36 us

profile of v1, /device:TPU:4, one launch (start us, length us, event | category | flops | bytes accessed | tf_op | source)
XLA Modules:
  0.0 88.7 jit_solution(769976153258866461)
XLA Ops:
  0.0 1.3 %reshape.17.mu_hbm = f32[1,384]{1,0:T(1,128)} reshape(bf16[384]{0:T(512)(128)(2,1)} %param.17) | data formatting | bytes 2304 | tf_op jit(solution)/shard_map/reshape | solution.py:265
  1.3 1.5 %reshape.18.lam_hbm = f32[384,1]{1,0:T(8,128)} reshape(bf16[384]{0:T(512)(128)(2,1)} %param.16) | data formatting | bytes 2304 | tf_op jit(solution)/shard_map/reshape | solution.py:264
  2.7 83.6 %shard_map.91 = f32[384,768]{1,0:T(8,128)} custom-call(f32[384,768]{1,0:T(8,128)} %c_hbm.1, bf16[384,768]{1,0:T(8,128)(2,1)} %a_hbm.1, bf16[384,768]{1,0:T(8,128)(2,1)} %b_hbm.1, bf16[384,384]{1,0:T(8,128)(2,1)} %u_hbm.1, bf16[384,384]{1,0:T(8,128)(2,1)} %p_hbm.1, bf16[384,384]{1,0:T(8,128)(2,1)} %v_hbm.1, bf16[384,384]{1,0:T(8,128)(2,1)} %q_hbm.1, ...), custom_call_target="tpu_custom_call" | custom-call | tf_op jit(solution)/shard_map/pallas_call | solution.py:267
  86.3 2.4 %copy.12 = f32[384,768]{1,0:T(8,128)} copy(f32[384,768]{1,0:T(8,128)} %shard_map.91) | data formatting | bytes 2359296

commit v2 on v1

v2 whole, which is shorter than its diff:
```python
import functools

import jax
import jax.numpy as jnp
from jax import lax
from jax.experimental import pallas as pl
from jax.experimental.pallas import tpu as pltpu
from jax.sharding import PartitionSpec as P

WAVES = 3
MEMBERS = 2
CHUNKS = 4
MESH = pl.DeviceIdType.MESH
f32 = jnp.float32
bf16 = jnp.bfloat16


def kernel(
    rows, cols, tile,
    c_hbm, a_hbm, b_hbm, u_hbm, p_hbm, v_hbm, q_hbm, val_hbm,
    out_hbm,
    state, abuf, bbuf, pbuf, ubuf, vbuf, qbuf, vals, xr, xc, part_one, part_three,
    load_sem, out_sem, go_sem,
    vq_send, vq_fsend, vq_recv,
    a_send, a_recv,
    b_send, b_fsend, b_recv,
    xr_send, xr_recv,
    xc_send, xc_recv,
):
    r = lax.axis_index("row")
    c = lax.axis_index("col")
    even_row = r % 2 == 0
    odd_row = r % 2 == 1
    even_col = c % 2 == 0
    mate = r + 1 - 2 * (r % 2)
    other = c + 2 - 4 * ((c // 2) % 2)
    chip_mate = c + 1 - 2 * (c % 2)
    step = tile // CHUNKS
    top = WAVES - 1

    def dot(left, right):
        return jnp.dot(left, right, preferred_element_type=f32)

    def part(ref, member):
        return ref.at[:, pl.ds(member * tile, tile)]

    loads = []

    def load(source, target):
        copy = pltpu.make_async_copy(source, target, load_sem.at[len(loads)])
        copy.start()
        loads.append(copy)
        return copy

    ld_p = load(p_hbm, pbuf)
    ld_c = [load(part(c_hbm, m), state.at[m]) for m in range(MEMBERS)]
    ld_val = load(val_hbm, vals.at[0])
    ld_u = load(u_hbm, ubuf)
    ld_a = [load(part(a_hbm, m), abuf.at[m]) for m in range(MEMBERS)]
    ld_v = load(v_hbm, vbuf.at[0])
    ld_q = load(q_hbm, qbuf.at[0])
    ld_b = [load(part(b_hbm, m), bbuf.at[0, m]) for m in range(MEMBERS)]

    barrier = pltpu.get_barrier_semaphore()
    count = jnp.int32(0)

    def greet(there, to):
        @pl.when(there)
        def _():
            pl.semaphore_signal(barrier, inc=1, device_id=to, device_id_type=MESH)

        return there.astype(jnp.int32)

    for d in (-2, -1, 1, 2):
        count += greet((r + d >= 0) & (r + d < rows), (r + d, c))
        count += greet((c + d >= 0) & (c + d < cols), (r, c + d))
    for d in (-2, 2):
        count += greet((r + d >= 0) & (r + d < rows), (r + d, other))
    pl.semaphore_wait(barrier, count)

    sends = []

    def remote(source, target, send, recv, to):
        return pltpu.make_async_remote_copy(
            src_ref=source, dst_ref=target, send_sem=send, recv_sem=recv,
            device_id=to, device_id_type=MESH,
        )

    def push(condition, *copy, keep=True):
        @pl.when(condition)
        def _():
            remote(*copy).start()

        if keep:
            sends.append((condition, copy))

    def got(target, recv):
        remote(target, target, recv, recv, (r, c)).wait_recv()

    def owns(s):
        j = r - s
        return (j >= 0) & (j // MEMBERS == c)

    home = r // MEMBERS
    away = home + 2 - 4 * ((home // 2) % 2)
    diagonal = c == home
    far = r + 2 < rows
    v_copy = (v_hbm, vbuf.at[2], vq_send.at[2, 0], vq_recv.at[2, 0], (r + 2, c))
    q_copy = (q_hbm, qbuf.at[2], vq_send.at[2, 1], vq_recv.at[2, 1], (r + 2, other))
    helper = c == away
    push(diagonal & far, val_hbm, vals.at[2], vq_send.at[2, 2], vq_recv.at[2, 2], (r + 2, c))
    push(diagonal & far, *v_copy, keep=False)
    push(helper & far, *q_copy, keep=False)
    near = diagonal & even_row & (r + 1 < rows)
    push(near, val_hbm, vals.at[1], vq_send.at[1, 2], vq_recv.at[1, 2], (r + 1, c))
    push(near, v_hbm, vbuf.at[1], vq_send.at[1, 0], vq_recv.at[1, 0], (r + 1, c))
    push(near, q_hbm, qbuf.at[1], vq_send.at[1, 1], vq_recv.at[1, 1], (r + 1, c))

    def push_b(t, m, early):
        l = MEMBERS * c + m
        reach = (l > r) & (r + t < rows)
        reach = reach & ((l <= r + 2) if early else (l > r + 2))
        if t == 1:
            reach = reach & even_row
        source, target = part(b_hbm, m), bbuf.at[t, m]
        push(reach, source, target, b_send.at[t, m], b_recv.at[t, m], (r + t, c))

    for m in range(MEMBERS):
        push_b(2, m, True)
    for m in range(MEMBERS):
        push_b(1, m, True)

    for copy in (ld_p, *ld_c, ld_val):
        copy.wait()
    m_top = jnp.clip(r - top - MEMBERS * c, 0, MEMBERS - 1)

    @pl.when(owns(top))
    def _():
        part_one[...] = dot(pbuf[...], state[m_top].astype(bf16)).astype(bf16)

    def release(condition, copy):
        @pl.when(condition)
        def _():
            remote(*copy).wait_send()
            pl.semaphore_signal(
                go_sem, inc=1, device_id=(r, chip_mate), device_id_type=MESH
            )

    release(diagonal & far, v_copy)
    release(helper & far, q_copy)

    @pl.when(((chip_mate == home) | (chip_mate == away)) & far)
    def _():
        pl.semaphore_wait(go_sem, 1)

    for m in range(MEMBERS):
        push(
            (c > 0) & (r < MEMBERS * c + m),
            part(a_hbm, m), abuf.at[MEMBERS + m], a_send.at[m], a_recv.at[m], (r, c - 1),
        )
    for t in (2, 1):
        for m in range(MEMBERS):
            push_b(t, m, False)

    def update_left(s, m, condition=None):
        i = MEMBERS * c + m + s
        below = (i < rows) & (r < i)
        if condition is not None:
            below = below & condition

        @pl.when(below)
        def _():
            state[m] = state[m] - dot(abuf[m + s], xc[s, m])

    def update_right(s, m, condition=None):
        right = (r - s >= 0) & (MEMBERS * c + m > r - s)
        if condition is not None:
            right = right & condition

        @pl.when(right)
        def _():
            state[m] = state[m] - dot(xr[s], bbuf[s, m])

    def rng(q):
        return pl.ds(q * step, step)

    def is_early(t, m):
        return MEMBERS * c + m <= r - t + 2

    def take_b(t, m, early):
        comes = (r - t >= 0) & (MEMBERS * c + m > r - t)
        comes = comes & (is_early(t, m) if early else jnp.logical_not(is_early(t, m)))

        @pl.when(comes)
        def _():
            got(bbuf.at[t, m], b_recv.at[t, m])

        return comes

    def take_far_b(early):
        for m in range(MEMBERS):
            comes = take_b(2, m, early)
            push(
                comes & odd_row, bbuf.at[2, m], bbuf.at[1, m],
                b_fsend.at[m], b_recv.at[1, m], (r - 1, c),
            )

    def own_member(s):
        return jnp.clip(r - s - MEMBERS * c, 0, MEMBERS - 1)

    def solve(s):
        mine = owns(s)
        m_own = own_member(s)

        @pl.when(mine)
        def _():
            if s < top:
                part_one[...] = dot(pbuf[...], state[m_own].astype(bf16)).astype(bf16)
            if s > 0:
                got(vbuf.at[s], vq_recv.at[s, 0])
                got(vals.at[s], vq_recv.at[s, 2])
            second = dot(part_one[...], vbuf[s])
            wide = jnp.transpose(jnp.broadcast_to(vals[0, 0:1, :], (128, tile)))
            divisor = wide[:, 0:1] + vals[s, 1:2, :]
            part_three[...] = (second / divisor).astype(bf16)
            if s > 0:
                got(qbuf.at[s], vq_recv.at[s, 1])

        half = tile // 2
        for k in range(2):
            @pl.when(mine)
            def _():
                span = pl.ds(k * half, half)
                third = dot(ubuf[span], part_three[...]).astype(bf16)
                solved = dot(third, qbuf[s])
                state[m_own, span] = solved
                xr[s, span] = solved.astype(bf16)

            for q in range(k * CHUNKS // 2, (k + 1) * CHUNKS // 2):
                lane = q % 2
                here = r % 2 == lane
                copy = (xr.at[s, rng(q)], xc.at[s, m_own, rng(q)])
                recv = xc_recv.at[s, m_own, q]
                push(
                    mine & here & (r >= 2),
                    *copy, xc_send.at[s, m_own, q, 0], recv, (r - 2, c),
                )
                push(
                    mine & (odd_row | (jnp.logical_not(here) & (r >= 2))),
                    *copy, xc_send.at[s, m_own, q, 1], recv, (mate, c),
                )
                pass_row(s, q, mine)

    def pass_row(s, q, condition):
        mine = owns(s)
        for d in (1, 2):
            reach = condition & (c + d < cols)
            reach = reach & (even_col if d == 2 else (even_col | mine))
            push(
                reach, xr.at[s, rng(q)], xr.at[s, rng(q)],
                xr_send.at[s, d - 1, q], xr_recv.at[s, q], (r, c + d),
                keep=False,
            )

    def arrivals(s):
        comes_row = (r - s >= 0) & (c > (r - s) // MEMBERS)
        for q in range(CHUNKS):
            @pl.when(comes_row)
            def _():
                got(xr.at[s, rng(q)], xr_recv.at[s, q])

            pass_row(s, q, comes_row)
        for m in range(MEMBERS):
            i = MEMBERS * c + m + s
            pair, source_pair = r // 2, i // 2
            lower = (i < rows) & (pair < source_pair)
            for q in list(range(0, CHUNKS, 1)):
                lane = q % 2
                here = r % 2 == lane
                beside = (i < rows) & (pair == source_pair) & (r != i)
                if lane == 0:
                    beside = beside & (r < i)
                else:
                    beside = beside & ((r < i) | (i >= 2))
                comes = lower | beside
                target = xc.at[s, m, rng(q)]

                @pl.when(comes)
                def _():
                    got(target, xc_recv.at[s, m, q])

                push(
                    comes & here & (r >= 2), target, target,
                    xc_send.at[s, m, q, 0], xc_recv.at[s, m, q], (r - 2, c), keep=False,
                )
                push(
                    lower & here, target, target,
                    xc_send.at[s, m, q, 1], xc_recv.at[s, m, q], (mate, c), keep=False,
                )

    def drain(s):
        mine = owns(s)
        held = (r - s >= 0) & (c >= (r - s) // MEMBERS)
        for q in range(CHUNKS):
            for d in (1, 2):
                reach = held & (c + d < cols)
                reach = reach & (even_col if d == 2 else (even_col | mine))

                @pl.when(reach)
                def _():
                    piece = xr.at[s, rng(q)]
                    remote(
                        piece, piece, xr_send.at[s, d - 1, q], xr_recv.at[s, q], (r, c)
                    ).wait_send()

            lane = q % 2
            here = r % 2 == lane
            for m in range(MEMBERS):
                i = MEMBERS * c + m + s
                pair, source_pair = r // 2, i // 2
                lower = (i < rows) & (pair < source_pair)
                beside = (i < rows) & (pair == source_pair) & (r != i)
                if lane == 0:
                    beside = beside & (r < i)
                else:
                    beside = beside & ((r < i) | (i >= 2))
                piece = xc.at[s, m, rng(q)]

                @pl.when((lower | beside) & here & (r >= 2))
                def _():
                    remote(
                        piece, piece, xc_send.at[s, m, q, 0], xc_recv.at[s, m, q], (r, c)
                    ).wait_send()

                @pl.when(lower & here)
                def _():
                    remote(
                        piece, piece, xc_send.at[s, m, q, 1], xc_recv.at[s, m, q], (r, c)
                    ).wait_send()

    def rest(s, m):
        return jnp.logical_not(owns(s - 1) & (own_member(s - 1) == m))

    ld_u.wait()
    solve(2)
    for k, slot in ((0, vbuf), (2, vals), (1, qbuf)):
        push(
            owns(2) & odd_row, slot.at[2], slot.at[1],
            vq_fsend.at[k], vq_recv.at[1, k], (r - 1, c),
        )
    arrivals(2)
    for copy in ld_a:
        copy.wait()
    for m in range(MEMBERS):
        @pl.when((c + 1 < cols) & (r < MEMBERS * (c + 1) + m))
        def _():
            got(abuf.at[MEMBERS + m], a_recv.at[m])
    take_far_b(True)
    update_left(2, own_member(1), owns(1))
    update_right(2, own_member(1), owns(1))
    solve(1)
    for m in range(MEMBERS):
        update_left(2, m, rest(2, m))
        update_right(2, m, rest(2, m) & is_early(2, m))
    arrivals(1)
    for m in range(MEMBERS):
        take_b(1, m, True)
    for copy in (ld_v, ld_q, *ld_b):
        copy.wait()
    update_left(1, own_member(0), owns(0))
    update_right(1, own_member(0), owns(0))
    solve(0)
    for m in range(MEMBERS):
        update_left(1, m, rest(1, m))
        update_right(1, m, rest(1, m) & is_early(1, m))
    take_far_b(False)
    for m in range(MEMBERS):
        update_right(2, m, jnp.logical_not(is_early(2, m)))
    arrivals(0)
    for m in range(MEMBERS):
        take_b(1, m, False)
    outs = []
    for m in range(MEMBERS):
        update_right(1, m, jnp.logical_not(is_early(1, m)))
        update_left(0, m)
        update_right(0, m)
        copy = pltpu.make_async_copy(state.at[m], part(out_hbm, m), out_sem.at[m])
        copy.start()
        outs.append(copy)
    for condition, copy in sends:
        @pl.when(condition)
        def _():
            remote(*copy).wait_send()
    for s in range(WAVES):
        drain(s)
    for copy in outs:
        copy.wait()


def shards(
    c_matrix, a_upper, b_upper, a_vectors, a_inverse, b_vectors, b_inverse, a_values, b_values
):
    tile = a_vectors.shape[1]
    rows = lax.axis_size("row")
    cols = lax.axis_size("col")
    values = jnp.stack([a_values, b_values]).astype(f32)
    dma = pltpu.SemaphoreType.DMA
    return pl.pallas_call(
        functools.partial(kernel, rows, cols, tile),
        out_shape=jax.ShapeDtypeStruct(c_matrix.shape, f32),
        in_specs=[pl.BlockSpec(memory_space=pl.ANY)] * 8,
        out_specs=pl.BlockSpec(memory_space=pl.ANY),
        scratch_shapes=[
            pltpu.VMEM((MEMBERS, tile, tile), f32),
            pltpu.VMEM((2 * MEMBERS, tile, tile), bf16),
            pltpu.VMEM((WAVES, MEMBERS, tile, tile), bf16),
            pltpu.VMEM((tile, tile), bf16),
            pltpu.VMEM((tile, tile), bf16),
            pltpu.VMEM((WAVES, tile, tile), bf16),
            pltpu.VMEM((WAVES, tile, tile), bf16),
            pltpu.VMEM((WAVES, 2, tile), f32),
            pltpu.VMEM((WAVES, tile, tile), bf16),
            pltpu.VMEM((WAVES, MEMBERS, tile, tile), bf16),
            pltpu.VMEM((tile, tile), bf16),
            pltpu.VMEM((tile, tile), bf16),
            dma((16,)), dma((MEMBERS,)), pltpu.SemaphoreType.REGULAR,
            dma((WAVES, 3)), dma((3,)), dma((WAVES, 3)),
            dma((MEMBERS,)), dma((MEMBERS,)),
            dma((WAVES, MEMBERS)), dma((MEMBERS,)), dma((WAVES, MEMBERS)),
            dma((WAVES, 2, CHUNKS)), dma((WAVES, CHUNKS)),
            dma((WAVES, MEMBERS, CHUNKS, 2)), dma((WAVES, MEMBERS, CHUNKS)),
        ],
        compiler_params=pltpu.CompilerParams(collective_id=0, has_side_effects=True),
    )(c_matrix, a_upper, b_upper, a_vectors, a_inverse, b_vectors, b_inverse, values)


def solution(mesh):
    placed = (
        P("row", "col"),
        P("row", "col"),
        P("row", "col"),
        P("row", None),
        P("row", None),
        P("row", None),
        P("row", None),
        P("row"),
        P("row"),
    )
    return jax.shard_map(
        shards, mesh=mesh, in_specs=placed, out_specs=P("row", "col"), check_vma=False
    )
```

time: 88.8 us -> 124 us (1.40)
  Pallas kernels: 83.6 us -> 119 us
  local copies, waits for them, and re-layouts: 5.08 us -> 3.72 us
    pallas_call x1, Pallas kernels: 83.6 us -> 119 us  [shards(): pl.pallas_call(functools.partial(kernel, rows, cols, tile), out_shape=jax...]
    reshape x2 -> x0, local copies, waits for them, and re-layouts: 2.72 us -> none  [the longest x1 1.47 us: shards(): lam = a_values.astype(f32).reshape(tile, 1)]
    another operation x0 -> x2, local copies, waits for them, and re-layouts: none -> 1.36 us  [shards(): values = jnp.stack([a_values, b_values]).astype(f32)]
where the time goes in v2:
time: 124 us
  Pallas kernels  119 us (96%)
  local copies, waits for them, and re-layouts  3.72 us (3%)
    pallas_call x1, Pallas kernels, shards(): pl.pallas_call(functools.partial(kernel, rows, cols, tile), out_shape=jax...  119 us

profile of v2, /device:TPU:4, one launch (start us, length us, event | category | flops | bytes accessed | tf_op | source)
XLA Modules:
  0.0 123.8 jit_solution(9733533821533031471)
XLA Ops:
  0.0 0.7 stack.9
  0.7 0.7 stack.10
  1.4 0.6 maximum_convert_fusion.val_hbm
  2.0 119.5 %shard_map.91 = f32[384,768]{1,0:T(8,128)} custom-call(f32[384,768]{1,0:T(8,128)} %c_hbm.1, bf16[384,768]{1,0:T(8,128)(2,1)} %a_hbm.1, bf16[384,768]{1,0:T(8,128)(2,1)} %b_hbm.1, bf16[384,384]{1,0:T(8,128)(2,1)} %u_hbm.1, bf16[384,384]{1,0:T(8,128)(2,1)} %p_hbm.1, bf16[384,384]{1,0:T(8,128)(2,1)} %v_hbm.1, bf16[384,384]{1,0:T(8,128)(2,1)} %q_hbm.1, ...), custom_call_target="tpu_custom_call" | custom-call | tf_op jit(solution)/shard_map/pallas_call | solution.py:408
  121.4 2.4 %copy.11 = f32[384,768]{1,0:T(8,128)} copy(f32[384,768]{1,0:T(8,128)} %shard_map.91) | data formatting | bytes 2359296

commit v3 on v2

--- a/solution.py
+++ b/solution.py
@@ -74,7 +74,6 @@
     for d in (-2, -1, 1, 2):
         count += greet((r + d >= 0) & (r + d < rows), (r + d, c))
         count += greet((c + d >= 0) & (c + d < cols), (r, c + d))
-    for d in (-2, 2):
         count += greet((r + d >= 0) & (r + d < rows), (r + d, other))
     pl.semaphore_wait(barrier, count)
 
@@ -111,6 +110,10 @@
     push(diagonal & far, val_hbm, vals.at[2], vq_send.at[2, 2], vq_recv.at[2, 2], (r + 2, c))
     push(diagonal & far, *v_copy, keep=False)
     push(helper & far, *q_copy, keep=False)
+    push(
+        helper & odd_row & (r + 1 < rows),
+        q_hbm, qbuf.at[1], vq_send.at[1, 1], vq_recv.at[1, 1], (r + 1, other),
+    )
     near = diagonal & even_row & (r + 1 < rows)
     push(near, val_hbm, vals.at[1], vq_send.at[1, 2], vq_recv.at[1, 2], (r + 1, c))
     push(near, v_hbm, vbuf.at[1], vq_send.at[1, 0], vq_recv.at[1, 0], (r + 1, c))
@@ -197,9 +200,16 @@
 
         return comes
 
+    comes_far = []
+
     def take_far_b(early):
         for m in range(MEMBERS):
             comes = take_b(2, m, early)
+            comes_far.append((m, comes))
+
+    def hand_b():
+        while comes_far:
+            m, comes = comes_far.pop(0)
             push(
                 comes & odd_row, bbuf.at[2, m], bbuf.at[1, m],
                 b_fsend.at[m], b_recv.at[1, m], (r - 1, c),
@@ -219,6 +229,16 @@
             if s > 0:
                 got(vbuf.at[s], vq_recv.at[s, 0])
                 got(vals.at[s], vq_recv.at[s, 2])
+
+        if s == top:
+            for k, slot in ((2, vals), (0, vbuf)):
+                push(
+                    mine & odd_row, slot.at[2], slot.at[1],
+                    vq_fsend.at[k], vq_recv.at[1, k], (r - 1, c),
+                )
+
+        @pl.when(mine)
+        def _():
             second = dot(part_one[...], vbuf[s])
             wide = jnp.transpose(jnp.broadcast_to(vals[0, 0:1, :], (128, tile)))
             divisor = wide[:, 0:1] + vals[s, 1:2, :]
@@ -270,33 +290,43 @@
                 got(xr.at[s, rng(q)], xr_recv.at[s, q])
 
             pass_row(s, q, comes_row)
-        for m in range(MEMBERS):
-            i = MEMBERS * c + m + s
-            pair, source_pair = r // 2, i // 2
-            lower = (i < rows) & (pair < source_pair)
-            for q in list(range(0, CHUNKS, 1)):
-                lane = q % 2
-                here = r % 2 == lane
-                beside = (i < rows) & (pair == source_pair) & (r != i)
-                if lane == 0:
-                    beside = beside & (r < i)
-                else:
-                    beside = beside & ((r < i) | (i >= 2))
-                comes = lower | beside
+        for q in range(CHUNKS):
+            for m in range(MEMBERS):
+                lower, beside, here = route(s, m, q)
                 target = xc.at[s, m, rng(q)]
 
-                @pl.when(comes)
+                @pl.when((lower | beside) & here)
                 def _():
                     got(target, xc_recv.at[s, m, q])
 
-                push(
-                    comes & here & (r >= 2), target, target,
-                    xc_send.at[s, m, q, 0], xc_recv.at[s, m, q], (r - 2, c), keep=False,
-                )
                 push(
                     lower & here, target, target,
                     xc_send.at[s, m, q, 1], xc_recv.at[s, m, q], (mate, c), keep=False,
                 )
+                push(
+                    (lower | beside) & here & (r >= 2), target, target,
+                    xc_send.at[s, m, q, 0], xc_recv.at[s, m, q], (r - 2, c), keep=False,
+                )
+
+    def settle(s):
+        for m in range(MEMBERS):
+            for q in range(CHUNKS):
+                lower, beside, here = route(s, m, q)
+
+                @pl.when((lower | beside) & jnp.logical_not(here))
+                def _():
+                    got(xc.at[s, m, rng(q)], xc_recv.at[s, m, q])
+
+    def route(s, m, q):
+        i = MEMBERS * c + m + s
+        pair, source_pair = r // 2, i // 2
+        lower = (i < rows) & (pair < source_pair)
+        beside = (i < rows) & (pair == source_pair) & (r != i)
+        if q % 2 == 0:
+            beside = beside & (r < i)
+        else:
+            beside = beside & ((r < i) | (i >= 2))
+        return lower, beside, r % 2 == q % 2
 
     def drain(s):
         mine = owns(s)
@@ -313,17 +343,8 @@
                         piece, piece, xr_send.at[s, d - 1, q], xr_recv.at[s, q], (r, c)
                     ).wait_send()
 
-            lane = q % 2
-            here = r % 2 == lane
             for m in range(MEMBERS):
-                i = MEMBERS * c + m + s
-                pair, source_pair = r // 2, i // 2
-                lower = (i < rows) & (pair < source_pair)
-                beside = (i < rows) & (pair == source_pair) & (r != i)
-                if lane == 0:
-                    beside = beside & (r < i)
-                else:
-                    beside = beside & ((r < i) | (i >= 2))
+                lower, beside, here = route(s, m, q)
                 piece = xc.at[s, m, rng(q)]
 
                 @pl.when((lower | beside) & here & (r >= 2))
@@ -343,11 +364,6 @@
 
     ld_u.wait()
     solve(2)
-    for k, slot in ((0, vbuf), (2, vals), (1, qbuf)):
-        push(
-            owns(2) & odd_row, slot.at[2], slot.at[1],
-            vq_fsend.at[k], vq_recv.at[1, k], (r - 1, c),
-        )
     arrivals(2)
     for copy in ld_a:
         copy.wait()
@@ -356,15 +372,20 @@
         def _():
             got(abuf.at[MEMBERS + m], a_recv.at[m])
     take_far_b(True)
+    settle(2)
     update_left(2, own_member(1), owns(1))
     update_right(2, own_member(1), owns(1))
     solve(1)
+    hand_b()
+    take_far_b(False)
+    hand_b()
     for m in range(MEMBERS):
         update_left(2, m, rest(2, m))
         update_right(2, m, rest(2, m) & is_early(2, m))
     arrivals(1)
     for m in range(MEMBERS):
         take_b(1, m, True)
+    settle(1)
     for copy in (ld_v, ld_q, *ld_b):
         copy.wait()
     update_left(1, own_member(0), owns(0))
@@ -373,12 +394,12 @@
     for m in range(MEMBERS):
         update_left(1, m, rest(1, m))
         update_right(1, m, rest(1, m) & is_early(1, m))
-    take_far_b(False)
     for m in range(MEMBERS):
         update_right(2, m, jnp.logical_not(is_early(2, m)))
     arrivals(0)
     for m in range(MEMBERS):
         take_b(1, m, False)
+    settle(0)
     outs = []
     for m in range(MEMBERS):
         update_right(1, m, jnp.logical_not(is_early(1, m)))

time: 124 us -> 74 us (0.60)
  the two profiles are of different devices: /device:TPU:4 before, /device:TPU:7 now
where the time goes in v3:
time: 74 us; the launch traced here: 73.8 us
  Pallas kernels  69.5 us (94%)
  local copies, waits for them, and re-layouts  3.72 us (5%)
    pallas_call x1, Pallas kernels, shards(): pl.pallas_call(functools.partial(kernel, rows, cols, tile), out_shape=jax...  69.5 us
    unnamed x1, local copies, waits for them, and re-layouts  2.36 us

profile of v3, /device:TPU:7, one launch (start us, length us, event | category | flops | bytes accessed | tf_op | source)
XLA Modules:
  0.0 73.8 jit_solution(15797842436498063595)
XLA Ops:
  0.0 0.7 stack.9
  0.7 0.7 stack.10
  1.4 0.6 maximum_convert_fusion.val_hbm
  2.0 69.5 %shard_map.91 = f32[384,768]{1,0:T(8,128)} custom-call(f32[384,768]{1,0:T(8,128)} %c_hbm.1, bf16[384,768]{1,0:T(8,128)(2,1)} %a_hbm.1, bf16[384,768]{1,0:T(8,128)(2,1)} %b_hbm.1, bf16[384,384]{1,0:T(8,128)(2,1)} %u_hbm.1, bf16[384,384]{1,0:T(8,128)(2,1)} %p_hbm.1, bf16[384,384]{1,0:T(8,128)(2,1)} %v_hbm.1, bf16[384,384]{1,0:T(8,128)(2,1)} %q_hbm.1, ...), custom_call_target="tpu_custom_call" | custom-call | tf_op jit(solution)/shard_map/pallas_call | solution.py:429
  71.4 2.4 %copy.11 = f32[384,768]{1,0:T(8,128)} copy(f32[384,768]{1,0:T(8,128)} %shard_map.91) | data formatting | bytes 2359296

commit v4 on v3

--- a/solution.py
+++ b/solution.py
@@ -128,11 +128,6 @@
         source, target = part(b_hbm, m), bbuf.at[t, m]
         push(reach, source, target, b_send.at[t, m], b_recv.at[t, m], (r + t, c))
 
-    for m in range(MEMBERS):
-        push_b(2, m, True)
-    for m in range(MEMBERS):
-        push_b(1, m, True)
-
     for copy in (ld_p, *ld_c, ld_val):
         copy.wait()
     m_top = jnp.clip(r - top - MEMBERS * c, 0, MEMBERS - 1)
@@ -156,6 +151,10 @@
     def _():
         pl.semaphore_wait(go_sem, 1)
 
+    for m in range(MEMBERS):
+        push_b(2, m, True)
+    for m in range(MEMBERS):
+        push_b(1, m, True)
     for m in range(MEMBERS):
         push(
             (c > 0) & (r < MEMBERS * c + m),

time: 74 us -> 73.3 us (level)
  no operation moved by 1% of the time
where the time goes in v4:
time: 73.3 us; the launch traced here: 73.1 us
  Pallas kernels  68.8 us (94%)
  local copies, waits for them, and re-layouts  3.72 us (5%)
    pallas_call x1, Pallas kernels, shards(): pl.pallas_call(functools.partial(kernel, rows, cols, tile), out_shape=jax...  68.8 us
    unnamed x1, local copies, waits for them, and re-layouts  2.36 us

profile of v4, /device:TPU:7, one launch (start us, length us, event | category | flops | bytes accessed | tf_op | source)
XLA Modules:
  0.0 73.1 jit_solution(3925886176307360407)
XLA Ops:
  0.0 0.7 stack.9
  0.7 0.7 stack.10
  1.4 0.6 maximum_convert_fusion.val_hbm
  2.0 68.8 %shard_map.91 = f32[384,768]{1,0:T(8,128)} custom-call(f32[384,768]{1,0:T(8,128)} %c_hbm.1, bf16[384,768]{1,0:T(8,128)(2,1)} %a_hbm.1, bf16[384,768]{1,0:T(8,128)(2,1)} %b_hbm.1, bf16[384,384]{1,0:T(8,128)(2,1)} %u_hbm.1, bf16[384,384]{1,0:T(8,128)(2,1)} %p_hbm.1, bf16[384,384]{1,0:T(8,128)(2,1)} %v_hbm.1, bf16[384,384]{1,0:T(8,128)(2,1)} %q_hbm.1, ...), custom_call_target="tpu_custom_call" | custom-call | tf_op jit(solution)/shard_map/pallas_call | solution.py:428
  70.8 2.4 %copy.11 = f32[384,768]{1,0:T(8,128)} copy(f32[384,768]{1,0:T(8,128)} %shard_map.91) | data formatting | bytes 2359296
